TPU v7x, 32 devices: a whole 2x2x4 slice. The times are simulated.
32 devices in a mesh: gx: 4 (over z), gy: 2 (over y), gz: 4 (over x, core).
Axes of the slice: x: 2, y: 2, z: 4, core: 2. Of those that a mesh axis runs over, the one named last changes fastest.
Arguments:
- pop_ratio: float32 [19, 8, 32, 512], P(None, 'gx', 'gy', 'gz'), may hold values from 0.7 to 1.3
- solid_flags: int32 [8, 32, 512], P('gx', 'gy', 'gz'), may hold values 0 or 1
- class_ids: int32 [8, 32, 512], P('gx', 'gy', 'gz'), may hold values from 0 to 7
- drag_table: float32 [8], replicated, may hold values from 0.05 to 1
- row_map: int32 [8, 32, 512], P('gx', 'gy', 'gz'), may hold values from 0 to 4095, as said below
- old_basis: float32 [32, 16384], P(None, ('gx', 'gy', 'gz')), may hold values from -6 to 6
- old_sigma: float32 [32], replicated, may hold values from 1 to 10
Outputs:
- final_populations: float32 [19, 8, 32, 512], P(None, 'gx', 'gy', 'gz')
- new_basis: float32 [44, 16384], P(None, ('gx', 'gy', 'gz'))
- triangle: float32 [44, 44], replicated
Inputs may be any that keep to these rules, and one draw needn't show every extreme that they name: `row_map`: within each slab along the first dimension every snapshot row is named by exactly 8 voxels, and the voxels of one device name rows of each block of 512 rows exactly 512 times.
All inputs are finite; a program needn't handle non-finite values. No bound on the sum of `solid_flags` on one device may be relied on, other than what follows from the above.
Results may differ from a plain program's by a relative error of at most 0.0003.
Values sent between devices are 32-bit elements; how exact they have to be, the bound alone decides.
No kernel may reach another device: no remote copies, remote signals or barrier semaphores. Data moves between devices by JAX's collectives and lax.ppermute only.
A program may use at most 64 MiB of HBM per device.

v0:
```python
import jax
import jax.numpy as jnp
import numpy as np
from jax import lax
from jax.sharding import PartitionSpec as P

STEPS = 4
VOX_ROW = 8
LATTICE = np.array(
    [
        [0, 0, 0],
        [1, 0, 0],
        [-1, 0, 0],
        [0, 1, 0],
        [0, -1, 0],
        [0, 0, 1],
        [0, 0, -1],
        [1, 1, 0],
        [-1, -1, 0],
        [1, -1, 0],
        [-1, 1, 0],
        [1, 0, 1],
        [-1, 0, -1],
        [1, 0, -1],
        [-1, 0, 1],
        [0, 1, 1],
        [0, -1, -1],
        [0, 1, -1],
        [0, -1, 1],
    ]
)
OPPOSITE = [0, 2, 1, 4, 3, 6, 5, 8, 7, 10, 9, 12, 11, 14, 13, 16, 15, 18, 17]
WEIGHTS = [1.0 / 3.0] + [1.0 / 18.0] * 6 + [1.0 / 36.0] * 12
relax_time = 0.9
vel_scale = 16.0


def extended(block, sides, width):
    for axis, dim in sides:
        count = lax.axis_size(axis)
        forward = [(i, i + 1) for i in range(count - 1)]
        forward.append((count - 1, 0))
        backward = [(target, source) for source, target in forward]
        low = lax.ppermute(
            lax.slice_in_dim(block, block.shape[dim] - width, None, axis=dim), axis, forward
        )
        high = lax.ppermute(lax.slice_in_dim(block, 0, width, axis=dim), axis, backward)
        block = jnp.concatenate([low, block, high], axis=dim)
    return block


def collide(populations, solid_flags, drag_rate):
    density = populations[0]
    for q in range(1, 19):
        density = density + populations[q]
    scale = 1.0 / (density * (1.0 + 0.5 * drag_rate))
    speeds = []
    for a in range(3):
        total = jnp.zeros_like(density)
        for q in range(19):
            if LATTICE[q, a] != 0:
                total = total + float(LATTICE[q, a]) * populations[q]
        speeds.append(total * scale)
    square = speeds[0] * speeds[0] + speeds[1] * speeds[1] + speeds[2] * speeds[2]
    relaxed = []
    for q in range(19):
        along = jnp.zeros_like(density)
        for a in range(3):
            if LATTICE[q, a] != 0:
                along = along + float(LATTICE[q, a]) * speeds[a]
        equilib = WEIGHTS[q] * density * (1.0 + 3.0 * along + 4.5 * along * along - 1.5 * square)
        relaxed.append(populations[q] - (populations[q] - equilib) / relax_time)
    relaxed = jnp.stack(relaxed)
    bounced = jnp.stack([populations[OPPOSITE[q]] for q in range(19)])
    result = jnp.where(solid_flags[None] == 1, bounced, relaxed)
    fluid_part = (1 - solid_flags).astype(jnp.float32)
    velocity = jnp.stack(speeds) * fluid_part[None]
    return (result, velocity)


def propagate(relaxed):
    padded = extended(relaxed, (("gx", 1), ("gy", 2), ("gz", 3)), 1)
    width_x, width_y, width_z = (relaxed.shape[1], relaxed.shape[2], relaxed.shape[3])
    moved = []
    for q in range(19):
        start_x = 1 - int(LATTICE[q, 0])
        start_y = 1 - int(LATTICE[q, 1])
        start_z = 1 - int(LATTICE[q, 2])
        moved.append(
            padded[
                q,
                start_x : start_x + width_x,
                start_y : start_y + width_y,
                start_z : start_z + width_z,
            ]
        )
    return jnp.stack(moved)


def on_device(pop_ratio, solid_flags, class_ids, drag_table, row_map, old_basis, old_sigma):
    weights = jnp.asarray(WEIGHTS, jnp.float32)
    populations = pop_ratio * weights[:, None, None, None]
    drag_rate = jnp.zeros(class_ids.shape, jnp.float32)
    for c in range(drag_table.shape[0]):
        drag_rate = drag_rate + jnp.where(class_ids == c, drag_table[c], 0.0)
    snaps = []
    for step in range(STEPS):
        relaxed, velocity = collide(populations, solid_flags, drag_rate)
        snaps.append(velocity.reshape(3, -1))
        populations = propagate(relaxed)
    values = jnp.concatenate(snaps, 0) * (vel_scale / VOX_ROW)
    cell_count = values.shape[1]
    rows_local = cell_count // VOX_ROW
    owners = lax.axis_size(("gy", "gz"))
    slab_rows = row_map.reshape(-1)
    term = jax.vmap(lambda v: jax.ops.segment_sum(v, slab_rows, num_segments=rows_local * owners))(
        values
    )
    snapshot = lax.psum_scatter(term, ("gy", "gz"), scatter_dimension=1, tiled=True)
    augmented = jnp.concatenate([old_sigma[:, None] * old_basis, snapshot], 0)
    total_rows = rows_local * lax.axis_size(("gx", "gy", "gz"))
    gram = jnp.dot(augmented, augmented.T, precision=lax.Precision.HIGHEST) / float(total_rows)
    total = lax.psum(gram, ("gx", "gy", "gz"))
    upper = jnp.linalg.cholesky(total).T
    new_basis = jax.scipy.linalg.solve_triangular(upper.T, augmented, lower=True)
    return (populations, new_basis, upper)


def solution(mesh):
    in_specs = (
        P(None, "gx", "gy", "gz"),
        P("gx", "gy", "gz"),
        P("gx", "gy", "gz"),
        P(),
        P("gx", "gy", "gz"),
        P(None, ("gx", "gy", "gz")),
        P(),
    )
    out_specs = (P(None, "gx", "gy", "gz"), P(None, ("gx", "gy", "gz")), P())
    return jax.shard_map(
        on_device, mesh=mesh, in_specs=in_specs, out_specs=out_specs, check_vma=False
    )
```

profile of v0, /device:TPU:0, one launch (start us, length us, event | category | flops | bytes accessed | tf_op | source)
XLA Modules:
  0.0 212.3 jit_solution(5937198158549665154)
XLA Ops:
  7.2 1.6 fusion.537
  8.8 1.1 broadcast_multiply_fusion
  9.9 0.7 broadcast_compare_fusion
  10.6 5.8 %constant_dynamic-update-slice_fusion.37 = (f32[19,2,16,128]{3,2,1,0:T(8,128)S(1)}, f32[2,16,128]{2,1,0:T(8,128)S(1)}, f32[2,16,128]{2,1,0:T(8,128)S(1)}, f32[2,...) fusion(f32[19,2,16,128]{3,2,1,0:T(8,128)S(1)} %broadcast_multiply_fus, ...), kind=kLoop, calls=%fused_computation.45 | loop fusion | flops 405503 | bytes 442400
  16.9 5.1 %collective-permute-start = (f32[19,1,16,128]{3,2,1,0:T(8,128)S(1)}, f32[19,1,16,128]{3,2,1,0:T(8,128)S(1)}, u32[]{:S(2)}, u32[]{:S(2)}) collective-permute-start(f32[19,1,16,128]{3,2,1,0:T(8,128)S(1)} %get-tuple-element.114), channel_id=1, source_target_pairs={{8,0},{16,8},{24,16},{0,24},{9,1},{17,9},{25,17},{1,25},{10,2},{18... | collective-permute-start | bytes 466952 | tf_op jit(solution)/shard_map/ppermute | solution.py:47
  22.1 4.4 %collective-permute-done = f32[19,1,16,128]{3,2,1,0:T(8,128)S(1)} collective-permute-done((f32[19,1,16,128]{3,2,1,0:T(8,128)S(1)}, f32[19,1,16,128]{3,2,1,0:T(8,128)S(1)}, u32[]{:S(2)}, u32[]{:S(2)}) %collective-permute-start) | collective-permute-done | bytes 155680 | tf_op jit(solution)/shard_map/ppermute | solution.py:47
  26.5 3.1 %collective-permute-done.1 = f32[19,1,16,128]{3,2,1,0:T(8,128)S(1)} collective-permute-done((f32[19,1,16,128]{3,2,1,0:T(8,128)S(1)}, f32[19,1,16,128]{3,2,1,0:T(8,128)S(1)}, u32[]{:S(2)}, u32[]{:S(2)}) %collective-permute-start.1) | collective-permute-done | bytes 155680 | tf_op jit(solution)/shard_map/ppermute | solution.py:44
  29.6 1.6 collective-permute-start.2
  31.7 2.0 collective-permute-done.2
  33.7 1.5 collective-permute-done.3
  35.7 0.6 copy.90
  36.3 0.6 copy.92
  36.9 0.5 collective-permute-start.5
  37.4 0.5 collective-permute-done.4
  37.9 1.0 copy.91
  39.0 1.3 collective-permute-done.5
  40.3 1.0 copy.93
  42.2 1.8 collective-permute-start.6
  44.2 4.3 %collective-permute-done.6 = f32[19,1,16,128]{3,2,1,0:T(8,128)S(1)} collective-permute-done((f32[19,1,16,128]{3,2,1,0:T(8,128)S(1)}, f32[19,1,16,128]{3,2,1,0:T(8,128)S(1)}, u32[]{:S(2)}, u32[]{:S(2)}) %collective-permute-start.6) | collective-permute-done | bytes 155680 | tf_op jit(solution)/shard_map/ppermute | solution.py:47
  48.5 3.6 %collective-permute-done.7 = f32[19,1,16,128]{3,2,1,0:T(8,128)S(1)} collective-permute-done((f32[19,1,16,128]{3,2,1,0:T(8,128)S(1)}, f32[19,1,16,128]{3,2,1,0:T(8,128)S(1)}, u32[]{:S(2)}, u32[]{:S(2)}) %collective-permute-start.7) | collective-permute-done | bytes 155680 | tf_op jit(solution)/shard_map/ppermute | solution.py:44
  52.1 0.6 collective-permute-start.8
  52.7 1.5 collective-permute-start.9
  54.2 2.0 collective-permute-done.8
  57.1 0.6 copy.94
  57.8 0.6 copy.96
  58.4 0.5 collective-permute-start.11
  58.9 0.5 collective-permute-done.10
  59.4 1.0 copy.95
  60.4 1.3 collective-permute-done.11
  61.8 1.0 copy.97
  63.7 2.3 %collective-permute-start.12 = (f32[19,1,16,128]{3,2,1,0:T(8,128)S(1)}, f32[19,1,16,128]{3,2,1,0:T(8,128)S(1)}, u32[]{:S(2)}, u32[]{:S(2)}) collective-permute-start(f32[19,1,16,128]{3,2,1,0:T(8,128)S(1)} %get-tuple-element.110), channel_id=1, source_target_pairs={{8,0},{16,8},{24,16},{0,24},{9,1},{17,9},{25,17},{1,25},{10,2},{18... | collective-permute-start | bytes 466952 | tf_op jit(solution)/shard_map/ppermute | solution.py:47
  66.1 4.3 %collective-permute-done.12 = f32[19,1,16,128]{3,2,1,0:T(8,128)S(1)} collective-permute-done((f32[19,1,16,128]{3,2,1,0:T(8,128)S(1)}, f32[19,1,16,128]{3,2,1,0:T(8,128)S(1)}, u32[]{:S(2)}, u32[]{:S(2)}) %collective-permute-start.12) | collective-permute-done | bytes 155680 | tf_op jit(solution)/shard_map/ppermute | solution.py:47
  70.4 3.7 %collective-permute-done.13 = f32[19,1,16,128]{3,2,1,0:T(8,128)S(1)} collective-permute-done((f32[19,1,16,128]{3,2,1,0:T(8,128)S(1)}, f32[19,1,16,128]{3,2,1,0:T(8,128)S(1)}, u32[]{:S(2)}, u32[]{:S(2)}) %collective-permute-start.13) | collective-permute-done | bytes 155680 | tf_op jit(solution)/shard_map/ppermute | solution.py:44
  74.2 1.6 collective-permute-start.14
  76.3 1.9 collective-permute-done.14
  78.2 1.5 collective-permute-done.15
  80.2 0.6 copy.98
  80.9 0.6 copy.100
  81.5 0.7 collective-permute-start.17
  82.5 1.1 copy.99
  83.6 1.5 collective-permute-done.17
  85.1 1.1 copy.101
  87.0 0.5 collective-permute-start.18
  87.5 3.3 %collective-permute-start.19 = (f32[19,1,16,128]{3,2,1,0:T(8,128)S(1)}, f32[19,1,16,128]{3,2,1,0:T(8,128)S(1)}, u32[]{:S(2)}, u32[]{:S(2)}) collective-permute-start(f32[19,1,16,128]{3,2,1,0:T(8,128)S(1)} %get-tuple-element.107), channel_id=1, source_target_pairs={{8,0},{16,8},{24,16},{0,24},{9,1},{17,9},{25,17},{1,25},{10,2},{18... | collective-permute-start | bytes 466952 | tf_op jit(solution)/shard_map/ppermute | solution.py:47
  91.1 0.6 copy.106
  91.8 23.9 %scatter_custom_fusion = f32[12,4096]{0,1:T(8,128)} fusion(s32[4096]{0:T(1024)} %bitcast.1436, f32[4096,12]{1,0:T(8,128)S(1)} %copy.106, f32[]{:T(128)} %constant.170.clone.1), kind=kCustom, calls=%fused_computation.2 | custom fusion | flops 49152 | bytes 197120 | tf_op jit(solution)/shard_map/vmap()/scatter-add | solution.py:116
  115.8 0.6 collective-permute-start.20
  116.4 1.5 collective-permute-start.21
  117.9 1.9 collective-permute-done.20
  120.8 0.7 copy.102
  121.5 0.7 copy.104
  122.2 1.7 collective-permute-start.23
  124.0 1.1 collective-permute-done.22
  125.0 0.6 copy.103
  125.7 0.6 copy.105
  127.1 27.1 %reduce-scatter.2.cloned.1.call-done = f32[12,512]{0,1:T(8,128)} async-done(((f32[12,4096]{0,1:T(8,128)}), f32[12,512]{0,1:T(8,128)}) %reduce-scatter.2.cloned.1.call-update) | async-done | bytes 24592 | tf_op jit(solution)/shard_map/reduce_scatter | solution.py:119
  154.2 1.1 copy.107
  155.5 39.5 %psum.7 = f32[44,44]{0,1:T(8,128)S(1)} all-reduce(f32[44,44]{0,1:T(8,128)S(1)} %convolution_multiply_fusion), channel_id=1, replica_groups=mesh['gx'=4,'gy'=2,'gz'=4] {'gx','gy','gz'}, use_global_device_ids=true, to_apply=%region_2.3 | all-reduce | flops 1936 | bytes 15488 | tf_op jit(solution)/shard_map/psum | solution.py:123
  195.1 4.0 %cholesky.16 = f32[44,44]{1,0:T(8,128)S(1)} custom-call(f32[44,44]{1,0:T(8,128)S(1)} %fusion.5), custom_call_target="Cholesky" | custom-call | tf_op jit(solution)/shard_map/jit(cholesky)/cholesky | solution.py:124
  199.2 0.6 compare_reduce_fusion
  199.8 0.7 fusion.6
  200.5 3.4 %custom-call.7 = f32[1,44,44]{1,2,0:T(8,128)S(1)} custom-call(f32[1,44,44]{2,1,0:T(8,128)S(1)} %get-tuple-element.152), custom_call_target="InvertDiagBlocksLowerTriangular" | custom-call | tf_op jit(solution)/shard_map/jit(_solve_triangular)/triangular_solve | solution.py:125
  203.9 0.9 fusion.3
  204.8 0.7 copy.110
  (177 shorter events, 8.8 us)
Async XLA Ops:
  7.2 147.1 %reduce-scatter.2.cloned.1.call-start = ((), (), s32[]{:S(2)}) async-start(), calls=%async_computation.1 | async-start | bytes 2359296 | tf_op jit(solution)/shard_map/reduce_scatter | solution.py:119
  16.9 9.5 %collective-permute-start = (f32[19,1,16,128]{3,2,1,0:T(8,128)S(1)}, f32[19,1,16,128]{3,2,1,0:T(8,128)S(1)}, u32[]{:S(2)}, u32[]{:S(2)}) collective-permute-start(f32[19,1,16,128]{3,2,1,0:T(8,128)S(1)} %get-tuple-element.114), channel_id=1, source_target_pairs={{8,0},{16,8},{24,16},{0,24},{9,1},{17,9},{25,17},{1,25},{10,2},{18... | collective-permute-start | bytes 466952 | tf_op jit(solution)/shard_map/ppermute | solution.py:47
  22.1 7.5 %collective-permute-start.1 = (f32[19,1,16,128]{3,2,1,0:T(8,128)S(1)}, f32[19,1,16,128]{3,2,1,0:T(8,128)S(1)}, u32[]{:S(2)}, u32[]{:S(2)}) collective-permute-start(f32[19,1,16,128]{3,2,1,0:T(8,128)S(1)} %get-tuple-element.113), channel_id=1, source_target_pairs={{0,8},{8,16},{16,24},{24,0},{1,9},{9,17},{17,25},{25,1},{2,10},{10... | collective-permute-start | bytes 466952 | tf_op jit(solution)/shard_map/ppermute | solution.py:44
  29.6 4.0 %collective-permute-start.2 = (f32[19,4,1,128]{3,2,1,0:T(1,128)S(1)}, f32[19,4,1,128]{3,2,1,0:T(1,128)S(1)}, u32[]{:S(2)}, u32[]{:S(2)}) collective-permute-start(f32[19,4,1,128]{3,2,1,0:T(1,128)S(1)} %get-tuple-element.106), channel_id=1, source_target_pairs={{4,0},{0,4},{5,1},{1,5},{6,2},{2,6},{7,3},{3,7},{12,8},{8,12},{13,... | collective-permute-start | bytes 116744 | tf_op jit(solution)/shard_map/ppermute | solution.py:47
  31.2 4.0 %collective-permute-start.3 = (f32[19,4,1,128]{3,2,1,0:T(1,128)S(1)}, f32[19,4,1,128]{3,2,1,0:T(1,128)S(1)}, u32[]{:S(2)}, u32[]{:S(2)}) collective-permute-start(f32[19,4,1,128]{3,2,1,0:T(1,128)S(1)} %get-tuple-element.105), channel_id=1, source_target_pairs={{0,4},{4,0},{1,5},{5,1},{2,6},{6,2},{3,7},{7,3},{8,12},{12,8},{9,1... | collective-permute-start | bytes 116744 | tf_op jit(solution)/shard_map/ppermute | solution.py:44
  36.3 1.7 collective-permute-start.4
  36.9 3.4 %collective-permute-start.5 = (f32[19,4,18,1]{0,1,3,2:T(4,128)S(1)}, f32[19,4,18,1]{0,1,3,2:T(4,128)S(1)}, u32[]{:S(2)}, u32[]{:S(2)}) collective-permute-start(f32[19,4,18,1]{0,1,3,2:T(4,128)S(1)} %copy.92), channel_id=1, source_target_pairs={{0,1},{1,2},{2,3},{3,0},{4,5},{5,6},{6,7},{7,4},{8,9},{9,10},{10,1... | collective-permute-start | bytes 16424 | tf_op jit(solution)/shard_map/ppermute | solution.py:44
  42.2 6.3 %collective-permute-start.6 = (f32[19,1,16,128]{3,2,1,0:T(8,128)S(1)}, f32[19,1,16,128]{3,2,1,0:T(8,128)S(1)}, u32[]{:S(2)}, u32[]{:S(2)}) collective-permute-start(f32[19,1,16,128]{3,2,1,0:T(8,128)S(1)} %get-tuple-element.112), channel_id=1, source_target_pairs={{8,0},{16,8},{24,16},{0,24},{9,1},{17,9},{25,17},{1,25},{10,2},{18... | collective-permute-start | bytes 466952 | tf_op jit(solution)/shard_map/ppermute | solution.py:47
  44.0 8.1 %collective-permute-start.7 = (f32[19,1,16,128]{3,2,1,0:T(8,128)S(1)}, f32[19,1,16,128]{3,2,1,0:T(8,128)S(1)}, u32[]{:S(2)}, u32[]{:S(2)}) collective-permute-start(f32[19,1,16,128]{3,2,1,0:T(8,128)S(1)} %get-tuple-element.111), channel_id=1, source_target_pairs={{0,8},{8,16},{16,24},{24,0},{1,9},{9,17},{17,25},{25,1},{2,10},{10... | collective-permute-start | bytes 466952 | tf_op jit(solution)/shard_map/ppermute | solution.py:44
  52.1 4.0 %collective-permute-start.8 = (f32[19,4,1,128]{3,2,1,0:T(1,128)S(1)}, f32[19,4,1,128]{3,2,1,0:T(1,128)S(1)}, u32[]{:S(2)}, u32[]{:S(2)}) collective-permute-start(f32[19,4,1,128]{3,2,1,0:T(1,128)S(1)} %get-tuple-element.104), channel_id=1, source_target_pairs={{4,0},{0,4},{5,1},{1,5},{6,2},{2,6},{7,3},{3,7},{12,8},{8,12},{13,... | collective-permute-start | bytes 116744 | tf_op jit(solution)/shard_map/ppermute | solution.py:47
  52.7 4.0 %collective-permute-start.9 = (f32[19,4,1,128]{3,2,1,0:T(1,128)S(1)}, f32[19,4,1,128]{3,2,1,0:T(1,128)S(1)}, u32[]{:S(2)}, u32[]{:S(2)}) collective-permute-start(f32[19,4,1,128]{3,2,1,0:T(1,128)S(1)} %get-tuple-element.103), channel_id=1, source_target_pairs={{0,4},{4,0},{1,5},{5,1},{2,6},{6,2},{3,7},{7,3},{8,12},{12,8},{9,1... | collective-permute-start | bytes 116744 | tf_op jit(solution)/shard_map/ppermute | solution.py:44
  57.7 1.7 collective-permute-start.10
  58.4 3.4 %collective-permute-start.11 = (f32[19,4,18,1]{0,1,3,2:T(4,128)S(1)}, f32[19,4,18,1]{0,1,3,2:T(4,128)S(1)}, u32[]{:S(2)}, u32[]{:S(2)}) collective-permute-start(f32[19,4,18,1]{0,1,3,2:T(4,128)S(1)} %copy.96), channel_id=1, source_target_pairs={{0,1},{1,2},{2,3},{3,0},{4,5},{5,6},{6,7},{7,4},{8,9},{9,10},{10,1... | collective-permute-start | bytes 16424 | tf_op jit(solution)/shard_map/ppermute | solution.py:44
  63.0 3.0 %copy-start.1 = (f32[32,512]{1,0:T(8,128)S(1)}, f32[32,512]{1,0:T(8,128)}, u32[]{:S(2)}) copy-start(f32[32,512]{1,0:T(8,128)} %param.13) | copy-start | bytes 196612
  63.0 2.9 %copy-start.3 = (f32[32]{0:T(128)S(1)}, f32[32]{0:T(128)}, u32[]{:S(2)}) copy-start(f32[32]{0:T(128)} %param.14) | copy-start | bytes 388
  63.1 13.1 %copy-start = (s32[2,16,128]{2,1,0:T(8,128)S(1)}, s32[2,16,128]{2,1,0:T(8,128)}, u32[]{:S(2)}) copy-start(s32[2,16,128]{2,1,0:T(8,128)} %param.9) | copy-start | bytes 49156
  63.7 6.7 %collective-permute-start.12 = (f32[19,1,16,128]{3,2,1,0:T(8,128)S(1)}, f32[19,1,16,128]{3,2,1,0:T(8,128)S(1)}, u32[]{:S(2)}, u32[]{:S(2)}) collective-permute-start(f32[19,1,16,128]{3,2,1,0:T(8,128)S(1)} %get-tuple-element.110), channel_id=1, source_target_pairs={{8,0},{16,8},{24,16},{0,24},{9,1},{17,9},{25,17},{1,25},{10,2},{18... | collective-permute-start | bytes 466952 | tf_op jit(solution)/shard_map/ppermute | solution.py:47
  66.0 8.2 %collective-permute-start.13 = (f32[19,1,16,128]{3,2,1,0:T(8,128)S(1)}, f32[19,1,16,128]{3,2,1,0:T(8,128)S(1)}, u32[]{:S(2)}, u32[]{:S(2)}) collective-permute-start(f32[19,1,16,128]{3,2,1,0:T(8,128)S(1)} %get-tuple-element.109), channel_id=1, source_target_pairs={{0,8},{8,16},{16,24},{24,0},{1,9},{9,17},{17,25},{25,1},{2,10},{10... | collective-permute-start | bytes 466952 | tf_op jit(solution)/shard_map/ppermute | solution.py:44
  74.2 4.0 %collective-permute-start.14 = (f32[19,4,1,128]{3,2,1,0:T(1,128)S(1)}, f32[19,4,1,128]{3,2,1,0:T(1,128)S(1)}, u32[]{:S(2)}, u32[]{:S(2)}) collective-permute-start(f32[19,4,1,128]{3,2,1,0:T(1,128)S(1)} %get-tuple-element.102), channel_id=1, source_target_pairs={{4,0},{0,4},{5,1},{1,5},{6,2},{2,6},{7,3},{3,7},{12,8},{8,12},{13,... | collective-permute-start | bytes 116744 | tf_op jit(solution)/shard_map/ppermute | solution.py:47
  75.8 4.0 %collective-permute-start.15 = (f32[19,4,1,128]{3,2,1,0:T(1,128)S(1)}, f32[19,4,1,128]{3,2,1,0:T(1,128)S(1)}, u32[]{:S(2)}, u32[]{:S(2)}) collective-permute-start(f32[19,4,1,128]{3,2,1,0:T(1,128)S(1)} %get-tuple-element.101), channel_id=1, source_target_pairs={{0,4},{4,0},{1,5},{5,1},{2,6},{6,2},{3,7},{7,3},{8,12},{12,8},{9,1... | collective-permute-start | bytes 116744 | tf_op jit(solution)/shard_map/ppermute | solution.py:44
  80.8 1.7 collective-permute-start.16
  81.5 3.6 %collective-permute-start.17 = (f32[19,4,18,1]{0,1,3,2:T(4,128)S(1)}, f32[19,4,18,1]{0,1,3,2:T(4,128)S(1)}, u32[]{:S(2)}, u32[]{:S(2)}) collective-permute-start(f32[19,4,18,1]{0,1,3,2:T(4,128)S(1)} %copy.100), channel_id=1, source_target_pairs={{0,1},{1,2},{2,3},{3,0},{4,5},{5,6},{6,7},{7,4},{8,9},{9,10},{10,1... | collective-permute-start | bytes 16424 | tf_op jit(solution)/shard_map/ppermute | solution.py:44
  87.0 28.7 %collective-permute-start.18 = (f32[19,1,16,128]{3,2,1,0:T(8,128)S(1)}, f32[19,1,16,128]{3,2,1,0:T(8,128)S(1)}, u32[]{:S(2)}, u32[]{:S(2)}) collective-permute-start(f32[19,1,16,128]{3,2,1,0:T(8,128)S(1)} %get-tuple-element.108), channel_id=1, source_target_pairs={{0,8},{8,16},{16,24},{24,0},{1,9},{9,17},{17,25},{25,1},{2,10},{10... | collective-permute-start | bytes 466952 | tf_op jit(solution)/shard_map/ppermute | solution.py:44
  87.5 28.2 %collective-permute-start.19 = (f32[19,1,16,128]{3,2,1,0:T(8,128)S(1)}, f32[19,1,16,128]{3,2,1,0:T(8,128)S(1)}, u32[]{:S(2)}, u32[]{:S(2)}) collective-permute-start(f32[19,1,16,128]{3,2,1,0:T(8,128)S(1)} %get-tuple-element.107), channel_id=1, source_target_pairs={{8,0},{16,8},{24,16},{0,24},{9,1},{17,9},{25,17},{1,25},{10,2},{18... | collective-permute-start | bytes 466952 | tf_op jit(solution)/shard_map/ppermute | solution.py:47
  115.8 4.0 %collective-permute-start.20 = (f32[19,4,1,128]{3,2,1,0:T(1,128)S(1)}, f32[19,4,1,128]{3,2,1,0:T(1,128)S(1)}, u32[]{:S(2)}, u32[]{:S(2)}) collective-permute-start(f32[19,4,1,128]{3,2,1,0:T(1,128)S(1)} %get-tuple-element.100), channel_id=1, source_target_pairs={{0,4},{4,0},{1,5},{5,1},{2,6},{6,2},{3,7},{7,3},{8,12},{12,8},{9,1... | collective-permute-start | bytes 116744 | tf_op jit(solution)/shard_map/ppermute | solution.py:44
  116.4 4.0 %collective-permute-start.21 = (f32[19,4,1,128]{3,2,1,0:T(1,128)S(1)}, f32[19,4,1,128]{3,2,1,0:T(1,128)S(1)}, u32[]{:S(2)}, u32[]{:S(2)}) collective-permute-start(f32[19,4,1,128]{3,2,1,0:T(1,128)S(1)} %get-tuple-element.99), channel_id=1, source_target_pairs={{4,0},{0,4},{5,1},{1,5},{6,2},{2,6},{7,3},{3,7},{12,8},{8,12},{13,... | collective-permute-start | bytes 116744 | tf_op jit(solution)/shard_map/ppermute | solution.py:47
  121.5 3.5 %collective-permute-start.22 = (f32[19,4,18,1]{2,0,3,1:T(8,128)S(1)}, f32[19,4,18,1]{2,0,3,1:T(8,128)S(1)}, u32[]{:S(2)}, u32[]{:S(2)}) collective-permute-start(f32[19,4,18,1]{2,0,3,1:T(8,128)S(1)} %copy.102), channel_id=1, source_target_pairs={{0,1},{1,2},{2,3},{3,0},{4,5},{5,6},{6,7},{7,4},{8,9},{9,10},{10,1... | collective-permute-start | bytes 16424 | tf_op jit(solution)/shard_map/ppermute | solution.py:44
  122.2 3.5 %collective-permute-start.23 = (f32[19,4,18,1]{2,0,3,1:T(8,128)S(1)}, f32[19,4,18,1]{2,0,3,1:T(8,128)S(1)}, u32[]{:S(2)}, u32[]{:S(2)}) collective-permute-start(f32[19,4,18,1]{2,0,3,1:T(8,128)S(1)} %copy.104), channel_id=1, source_target_pairs={{1,0},{2,1},{3,2},{0,3},{5,4},{6,5},{7,6},{4,7},{9,8},{10,9},{11,1... | collective-permute-start | bytes 16424 | tf_op jit(solution)/shard_map/ppermute | solution.py:47
  127.1 78.4 %copy-start.2 = (f32[19,2,16,128]{3,2,1,0:T(8,128)}, f32[19,2,16,128]{3,2,1,0:T(8,128)S(1)}, u32[]{:S(2)}) copy-start(f32[19,2,16,128]{3,2,1,0:T(8,128)S(1)} %constant_dynamic-update-slice_fusion.152) | copy-start | bytes 933892
Sparse Core Ops, SparseCore 0:
  115.8 38.3 reduce-scatter.1
where the time goes:
time: 213 us; the launch traced here: 212 us
  waiting for transfers between devices  69 us (32%)
  other arithmetic  44.2 us (21%)
  blocking collectives  39.5 us (19%)
  starting transfers between devices  25.4 us (12%)
  local copies, waits for them, and re-layouts  18 us (8%)
  between operations  15 us (7%)
    psum x1, blocking collectives, on_device(): total = lax.psum(gram, ('gx', 'gy', 'gz'))  39.5 us
    reduce_scatter x1, waiting for transfers between devices, on_device(): lax.psum_scatter(term, ('gy', 'gz'), scatter_dimension=1, tiled=True)  27.1 us
    scatter-add x1, other arithmetic, on_device(): jax.ops.segment_sum(v, slab_rows, num_segments=rows_local * owners)  23.9 us
    ppermute x12, waiting for transfers between devices, extended(): lax.ppermute(lax.slice_in_dim(block, block.shape[dim] - width, None, axis...  21.1 us
    ppermute x12, waiting for transfers between devices, extended(): lax.ppermute(lax.slice_in_dim(block, 0, width, axis=dim), axis, backward)  20.8 us
    ppermute x12, starting transfers between devices, extended(): lax.ppermute(lax.slice_in_dim(block, 0, width, axis=dim), axis, backward)  19.7 us
    unnamed x89, other arithmetic  8.3 us
    ppermute x12, starting transfers between devices, extended(): lax.ppermute(lax.slice_in_dim(block, block.shape[dim] - width, None, axis...  5.69 us
  transfers between devices with their start and end apart: 25, of which 23 were waited for; matrix products, arithmetic and copies ran while one was open for 16% of the time, Pallas kernels for 0%

commit v1 on v0

--- a/solution.py
+++ b/solution.py
@@ -120,7 +120,7 @@
     augmented = jnp.concatenate([old_sigma[:, None] * old_basis, snapshot], 0)
     total_rows = rows_local * lax.axis_size(("gx", "gy", "gz"))
     gram = jnp.dot(augmented, augmented.T, precision=lax.Precision.HIGHEST) / float(total_rows)
-    total = lax.psum(gram, ("gx", "gy", "gz"))
+    total = jnp.sum(lax.all_gather(gram, ("gx", "gy", "gz")), axis=0)
     upper = jnp.linalg.cholesky(total).T
     new_basis = jax.scipy.linalg.solve_triangular(upper.T, augmented, lower=True)
     return (populations, new_basis, upper)

time: 213 us -> 216 us (1.014)
  blocking collectives: 39.5 us -> 42.7 us
    all_gather x0 -> x1, blocking collectives: none -> 42.7 us  [on_device(): total = jnp.sum(lax.all_gather(gram, ('gx', 'gy', 'gz')), axis=0)]
    psum x1 -> x0, blocking collectives: 39.5 us -> none  [on_device(): total = lax.psum(gram, ('gx', 'gy', 'gz'))]
where the time goes in v1:
time: 216 us
  waiting for transfers between devices  69 us (32%)
  other arithmetic  44.3 us (21%)
  blocking collectives  42.7 us (20%)
  starting transfers between devices  25.4 us (12%)
  local copies, waits for them, and re-layouts  18 us (8%)
  between operations  15 us (7%)
    all_gather x1, blocking collectives, on_device(): total = jnp.sum(lax.all_gather(gram, ('gx', 'gy', 'gz')), axis=0)  42.7 us
    reduce_scatter x1, waiting for transfers between devices, on_device(): lax.psum_scatter(term, ('gy', 'gz'), scatter_dimension=1, tiled=True)  27.1 us
    scatter-add x1, other arithmetic, on_device(): jax.ops.segment_sum(v, slab_rows, num_segments=rows_local * owners)  23.9 us
    ppermute x12, waiting for transfers between devices, extended(): lax.ppermute(lax.slice_in_dim(block, block.shape[dim] - width, None, axis...  21.1 us
    ppermute x12, waiting for transfers between devices, extended(): lax.ppermute(lax.slice_in_dim(block, 0, width, axis=dim), axis, backward)  20.8 us
    ppermute x12, starting transfers between devices, extended(): lax.ppermute(lax.slice_in_dim(block, 0, width, axis=dim), axis, backward)  19.7 us
    unnamed x89, other arithmetic  8.3 us
    ppermute x12, starting transfers between devices, extended(): lax.ppermute(lax.slice_in_dim(block, block.shape[dim] - width, None, axis...  5.69 us
  transfers between devices with their start and end apart: 25, of which 23 were waited for; matrix products, arithmetic and copies ran while one was open for 16% of the time, Pallas kernels for 0%

profile of v1, /device:TPU:0, one launch (start us, length us, event | category | flops | bytes accessed | tf_op | source)
XLA Modules:
  0.0 215.6 jit_solution(13114048192198215583)
XLA Ops:
  7.2 1.6 fusion.538
  8.8 1.1 broadcast_multiply_fusion
  9.9 0.7 broadcast_compare_fusion
  10.6 5.8 %constant_dynamic-update-slice_fusion.37 = (f32[19,2,16,128]{3,2,1,0:T(8,128)S(1)}, f32[2,16,128]{2,1,0:T(8,128)S(1)}, f32[2,16,128]{2,1,0:T(8,128)S(1)}, f32[2,...) fusion(f32[19,2,16,128]{3,2,1,0:T(8,128)S(1)} %broadcast_multiply_fus, ...), kind=kLoop, calls=%fused_computation.46 | loop fusion | flops 405503 | bytes 442400
  16.9 5.1 %collective-permute-start = (f32[19,1,16,128]{3,2,1,0:T(8,128)S(1)}, f32[19,1,16,128]{3,2,1,0:T(8,128)S(1)}, u32[]{:S(2)}, u32[]{:S(2)}) collective-permute-start(f32[19,1,16,128]{3,2,1,0:T(8,128)S(1)} %get-tuple-element.114), channel_id=1, source_target_pairs={{8,0},{16,8},{24,16},{0,24},{9,1},{17,9},{25,17},{1,25},{10,2},{18... | collective-permute-start | bytes 466952 | tf_op jit(solution)/shard_map/ppermute | solution.py:47
  22.1 4.4 %collective-permute-done = f32[19,1,16,128]{3,2,1,0:T(8,128)S(1)} collective-permute-done((f32[19,1,16,128]{3,2,1,0:T(8,128)S(1)}, f32[19,1,16,128]{3,2,1,0:T(8,128)S(1)}, u32[]{:S(2)}, u32[]{:S(2)}) %collective-permute-start) | collective-permute-done | bytes 155680 | tf_op jit(solution)/shard_map/ppermute | solution.py:47
  26.5 3.1 %collective-permute-done.1 = f32[19,1,16,128]{3,2,1,0:T(8,128)S(1)} collective-permute-done((f32[19,1,16,128]{3,2,1,0:T(8,128)S(1)}, f32[19,1,16,128]{3,2,1,0:T(8,128)S(1)}, u32[]{:S(2)}, u32[]{:S(2)}) %collective-permute-start.1) | collective-permute-done | bytes 155680 | tf_op jit(solution)/shard_map/ppermute | solution.py:44
  29.6 1.6 collective-permute-start.2
  31.7 2.0 collective-permute-done.2
  33.7 1.5 collective-permute-done.3
  35.7 0.6 copy.88
  36.3 0.6 copy.90
  36.9 0.5 collective-permute-start.5
  37.4 0.5 collective-permute-done.4
  37.9 1.0 copy.89
  39.0 1.3 collective-permute-done.5
  40.3 1.0 copy.91
  42.2 1.8 collective-permute-start.6
  44.2 4.3 %collective-permute-done.6 = f32[19,1,16,128]{3,2,1,0:T(8,128)S(1)} collective-permute-done((f32[19,1,16,128]{3,2,1,0:T(8,128)S(1)}, f32[19,1,16,128]{3,2,1,0:T(8,128)S(1)}, u32[]{:S(2)}, u32[]{:S(2)}) %collective-permute-start.6) | collective-permute-done | bytes 155680 | tf_op jit(solution)/shard_map/ppermute | solution.py:47
  48.5 3.6 %collective-permute-done.7 = f32[19,1,16,128]{3,2,1,0:T(8,128)S(1)} collective-permute-done((f32[19,1,16,128]{3,2,1,0:T(8,128)S(1)}, f32[19,1,16,128]{3,2,1,0:T(8,128)S(1)}, u32[]{:S(2)}, u32[]{:S(2)}) %collective-permute-start.7) | collective-permute-done | bytes 155680 | tf_op jit(solution)/shard_map/ppermute | solution.py:44
  52.1 0.6 collective-permute-start.8
  52.7 1.5 collective-permute-start.9
  54.2 2.0 collective-permute-done.8
  57.1 0.6 copy.92
  57.8 0.6 copy.94
  58.4 0.5 collective-permute-start.11
  58.9 0.5 collective-permute-done.10
  59.4 1.0 copy.93
  60.4 1.3 collective-permute-done.11
  61.8 1.0 copy.95
  63.7 2.3 %collective-permute-start.12 = (f32[19,1,16,128]{3,2,1,0:T(8,128)S(1)}, f32[19,1,16,128]{3,2,1,0:T(8,128)S(1)}, u32[]{:S(2)}, u32[]{:S(2)}) collective-permute-start(f32[19,1,16,128]{3,2,1,0:T(8,128)S(1)} %get-tuple-element.110), channel_id=1, source_target_pairs={{8,0},{16,8},{24,16},{0,24},{9,1},{17,9},{25,17},{1,25},{10,2},{18... | collective-permute-start | bytes 466952 | tf_op jit(solution)/shard_map/ppermute | solution.py:47
  66.1 4.3 %collective-permute-done.12 = f32[19,1,16,128]{3,2,1,0:T(8,128)S(1)} collective-permute-done((f32[19,1,16,128]{3,2,1,0:T(8,128)S(1)}, f32[19,1,16,128]{3,2,1,0:T(8,128)S(1)}, u32[]{:S(2)}, u32[]{:S(2)}) %collective-permute-start.12) | collective-permute-done | bytes 155680 | tf_op jit(solution)/shard_map/ppermute | solution.py:47
  70.4 3.7 %collective-permute-done.13 = f32[19,1,16,128]{3,2,1,0:T(8,128)S(1)} collective-permute-done((f32[19,1,16,128]{3,2,1,0:T(8,128)S(1)}, f32[19,1,16,128]{3,2,1,0:T(8,128)S(1)}, u32[]{:S(2)}, u32[]{:S(2)}) %collective-permute-start.13) | collective-permute-done | bytes 155680 | tf_op jit(solution)/shard_map/ppermute | solution.py:44
  74.2 1.6 collective-permute-start.14
  76.3 1.9 collective-permute-done.14
  78.2 1.5 collective-permute-done.15
  80.2 0.6 copy.96
  80.9 0.6 copy.98
  81.5 0.7 collective-permute-start.17
  82.5 1.1 copy.97
  83.6 1.5 collective-permute-done.17
  85.1 1.1 copy.99
  87.0 0.5 collective-permute-start.18
  87.5 3.3 %collective-permute-start.19 = (f32[19,1,16,128]{3,2,1,0:T(8,128)S(1)}, f32[19,1,16,128]{3,2,1,0:T(8,128)S(1)}, u32[]{:S(2)}, u32[]{:S(2)}) collective-permute-start(f32[19,1,16,128]{3,2,1,0:T(8,128)S(1)} %get-tuple-element.107), channel_id=1, source_target_pairs={{8,0},{16,8},{24,16},{0,24},{9,1},{17,9},{25,17},{1,25},{10,2},{18... | collective-permute-start | bytes 466952 | tf_op jit(solution)/shard_map/ppermute | solution.py:47
  91.1 0.6 copy.104
  91.8 23.9 %scatter_custom_fusion = f32[12,4096]{0,1:T(8,128)} fusion(s32[4096]{0:T(1024)} %bitcast.1438, f32[4096,12]{1,0:T(8,128)S(1)} %copy.104, f32[]{:T(128)} %constant.170.clone.1), kind=kCustom, calls=%fused_computation.3 | custom fusion | flops 49152 | bytes 197120 | tf_op jit(solution)/shard_map/vmap()/scatter-add | solution.py:116
  115.8 0.6 collective-permute-start.20
  116.4 1.5 collective-permute-start.21
  117.9 1.9 collective-permute-done.20
  120.8 0.7 copy.100
  121.5 0.7 copy.102
  122.2 1.7 collective-permute-start.23
  124.0 1.1 collective-permute-done.22
  125.0 0.6 copy.101
  125.7 0.6 copy.103
  127.1 27.1 %reduce-scatter.2.cloned.1.call-done = f32[12,512]{0,1:T(8,128)} async-done(((f32[12,4096]{0,1:T(8,128)}), f32[12,512]{0,1:T(8,128)}) %reduce-scatter.2.cloned.1.call-update) | async-done | bytes 24592 | tf_op jit(solution)/shard_map/reduce_scatter | solution.py:119
  154.2 1.1 copy.105
  155.5 42.7 %all-gather.1 = f32[32,44,44]{2,1,0:T(8,128)S(1)} all-gather(f32[1,44,44]{2,1,0:T(8,128)S(1)} %fusion), channel_id=2, replica_groups=mesh['gx'=4,'gy'=2,'gz'=4] {'gx','gy','gz'}, dimensions={0}, use_global_device_ids=true | all-gather | bytes 255552 | tf_op jit(solution)/shard_map/all_gather | solution.py:123
  198.4 4.0 %cholesky.16 = f32[44,44]{1,0:T(8,128)S(1)} custom-call(f32[44,44]{1,0:T(8,128)S(1)} %fusion.6), custom_call_target="Cholesky" | custom-call | tf_op jit(solution)/shard_map/jit(cholesky)/cholesky | solution.py:124
  202.4 0.6 compare_reduce_fusion
  203.1 0.7 fusion.7
  203.7 3.4 %custom-call.7 = f32[1,44,44]{1,2,0:T(8,128)S(1)} custom-call(f32[1,44,44]{2,1,0:T(8,128)S(1)} %get-tuple-element.152), custom_call_target="InvertDiagBlocksLowerTriangular" | custom-call | tf_op jit(solution)/shard_map/jit(_solve_triangular)/triangular_solve | solution.py:125
  207.1 0.9 fusion.4
  208.0 0.7 copy.107
  (178 shorter events, 8.9 us)
Async XLA Ops:
  7.2 147.1 %reduce-scatter.2.cloned.1.call-start = ((), (), s32[]{:S(2)}) async-start(), calls=%async_computation.1 | async-start | bytes 2359296 | tf_op jit(solution)/shard_map/reduce_scatter | solution.py:119
  16.9 9.5 %collective-permute-start = (f32[19,1,16,128]{3,2,1,0:T(8,128)S(1)}, f32[19,1,16,128]{3,2,1,0:T(8,128)S(1)}, u32[]{:S(2)}, u32[]{:S(2)}) collective-permute-start(f32[19,1,16,128]{3,2,1,0:T(8,128)S(1)} %get-tuple-element.114), channel_id=1, source_target_pairs={{8,0},{16,8},{24,16},{0,24},{9,1},{17,9},{25,17},{1,25},{10,2},{18... | collective-permute-start | bytes 466952 | tf_op jit(solution)/shard_map/ppermute | solution.py:47
  22.1 7.5 %collective-permute-start.1 = (f32[19,1,16,128]{3,2,1,0:T(8,128)S(1)}, f32[19,1,16,128]{3,2,1,0:T(8,128)S(1)}, u32[]{:S(2)}, u32[]{:S(2)}) collective-permute-start(f32[19,1,16,128]{3,2,1,0:T(8,128)S(1)} %get-tuple-element.113), channel_id=1, source_target_pairs={{0,8},{8,16},{16,24},{24,0},{1,9},{9,17},{17,25},{25,1},{2,10},{10... | collective-permute-start | bytes 466952 | tf_op jit(solution)/shard_map/ppermute | solution.py:44
  29.6 4.0 %collective-permute-start.2 = (f32[19,4,1,128]{3,2,1,0:T(1,128)S(1)}, f32[19,4,1,128]{3,2,1,0:T(1,128)S(1)}, u32[]{:S(2)}, u32[]{:S(2)}) collective-permute-start(f32[19,4,1,128]{3,2,1,0:T(1,128)S(1)} %get-tuple-element.106), channel_id=1, source_target_pairs={{4,0},{0,4},{5,1},{1,5},{6,2},{2,6},{7,3},{3,7},{12,8},{8,12},{13,... | collective-permute-start | bytes 116744 | tf_op jit(solution)/shard_map/ppermute | solution.py:47
  31.2 4.0 %collective-permute-start.3 = (f32[19,4,1,128]{3,2,1,0:T(1,128)S(1)}, f32[19,4,1,128]{3,2,1,0:T(1,128)S(1)}, u32[]{:S(2)}, u32[]{:S(2)}) collective-permute-start(f32[19,4,1,128]{3,2,1,0:T(1,128)S(1)} %get-tuple-element.105), channel_id=1, source_target_pairs={{0,4},{4,0},{1,5},{5,1},{2,6},{6,2},{3,7},{7,3},{8,12},{12,8},{9,1... | collective-permute-start | bytes 116744 | tf_op jit(solution)/shard_map/ppermute | solution.py:44
  36.3 1.7 collective-permute-start.4
  36.9 3.4 %collective-permute-start.5 = (f32[19,4,18,1]{0,1,3,2:T(4,128)S(1)}, f32[19,4,18,1]{0,1,3,2:T(4,128)S(1)}, u32[]{:S(2)}, u32[]{:S(2)}) collective-permute-start(f32[19,4,18,1]{0,1,3,2:T(4,128)S(1)} %copy.90), channel_id=1, source_target_pairs={{0,1},{1,2},{2,3},{3,0},{4,5},{5,6},{6,7},{7,4},{8,9},{9,10},{10,1... | collective-permute-start | bytes 16424 | tf_op jit(solution)/shard_map/ppermute | solution.py:44
  42.2 6.3 %collective-permute-start.6 = (f32[19,1,16,128]{3,2,1,0:T(8,128)S(1)}, f32[19,1,16,128]{3,2,1,0:T(8,128)S(1)}, u32[]{:S(2)}, u32[]{:S(2)}) collective-permute-start(f32[19,1,16,128]{3,2,1,0:T(8,128)S(1)} %get-tuple-element.112), channel_id=1, source_target_pairs={{8,0},{16,8},{24,16},{0,24},{9,1},{17,9},{25,17},{1,25},{10,2},{18... | collective-permute-start | bytes 466952 | tf_op jit(solution)/shard_map/ppermute | solution.py:47
  44.0 8.1 %collective-permute-start.7 = (f32[19,1,16,128]{3,2,1,0:T(8,128)S(1)}, f32[19,1,16,128]{3,2,1,0:T(8,128)S(1)}, u32[]{:S(2)}, u32[]{:S(2)}) collective-permute-start(f32[19,1,16,128]{3,2,1,0:T(8,128)S(1)} %get-tuple-element.111), channel_id=1, source_target_pairs={{0,8},{8,16},{16,24},{24,0},{1,9},{9,17},{17,25},{25,1},{2,10},{10... | collective-permute-start | bytes 466952 | tf_op jit(solution)/shard_map/ppermute | solution.py:44
  52.1 4.0 %collective-permute-start.8 = (f32[19,4,1,128]{3,2,1,0:T(1,128)S(1)}, f32[19,4,1,128]{3,2,1,0:T(1,128)S(1)}, u32[]{:S(2)}, u32[]{:S(2)}) collective-permute-start(f32[19,4,1,128]{3,2,1,0:T(1,128)S(1)} %get-tuple-element.104), channel_id=1, source_target_pairs={{4,0},{0,4},{5,1},{1,5},{6,2},{2,6},{7,3},{3,7},{12,8},{8,12},{13,... | collective-permute-start | bytes 116744 | tf_op jit(solution)/shard_map/ppermute | solution.py:47
  52.7 4.0 %collective-permute-start.9 = (f32[19,4,1,128]{3,2,1,0:T(1,128)S(1)}, f32[19,4,1,128]{3,2,1,0:T(1,128)S(1)}, u32[]{:S(2)}, u32[]{:S(2)}) collective-permute-start(f32[19,4,1,128]{3,2,1,0:T(1,128)S(1)} %get-tuple-element.103), channel_id=1, source_target_pairs={{0,4},{4,0},{1,5},{5,1},{2,6},{6,2},{3,7},{7,3},{8,12},{12,8},{9,1... | collective-permute-start | bytes 116744 | tf_op jit(solution)/shard_map/ppermute | solution.py:44
  57.7 1.7 collective-permute-start.10
  58.4 3.4 %collective-permute-start.11 = (f32[19,4,18,1]{0,1,3,2:T(4,128)S(1)}, f32[19,4,18,1]{0,1,3,2:T(4,128)S(1)}, u32[]{:S(2)}, u32[]{:S(2)}) collective-permute-start(f32[19,4,18,1]{0,1,3,2:T(4,128)S(1)} %copy.94), channel_id=1, source_target_pairs={{0,1},{1,2},{2,3},{3,0},{4,5},{5,6},{6,7},{7,4},{8,9},{9,10},{10,1... | collective-permute-start | bytes 16424 | tf_op jit(solution)/shard_map/ppermute | solution.py:44
  63.0 3.0 %copy-start.1 = (f32[32,512]{1,0:T(8,128)S(1)}, f32[32,512]{1,0:T(8,128)}, u32[]{:S(2)}) copy-start(f32[32,512]{1,0:T(8,128)} %param.13) | copy-start | bytes 196612
  63.0 2.9 %copy-start.3 = (f32[32]{0:T(128)S(1)}, f32[32]{0:T(128)}, u32[]{:S(2)}) copy-start(f32[32]{0:T(128)} %param.14) | copy-start | bytes 388
  63.1 13.1 %copy-start = (s32[2,16,128]{2,1,0:T(8,128)S(1)}, s32[2,16,128]{2,1,0:T(8,128)}, u32[]{:S(2)}) copy-start(s32[2,16,128]{2,1,0:T(8,128)} %param.9) | copy-start | bytes 49156
  63.7 6.7 %collective-permute-start.12 = (f32[19,1,16,128]{3,2,1,0:T(8,128)S(1)}, f32[19,1,16,128]{3,2,1,0:T(8,128)S(1)}, u32[]{:S(2)}, u32[]{:S(2)}) collective-permute-start(f32[19,1,16,128]{3,2,1,0:T(8,128)S(1)} %get-tuple-element.110), channel_id=1, source_target_pairs={{8,0},{16,8},{24,16},{0,24},{9,1},{17,9},{25,17},{1,25},{10,2},{18... | collective-permute-start | bytes 466952 | tf_op jit(solution)/shard_map/ppermute | solution.py:47
  66.0 8.2 %collective-permute-start.13 = (f32[19,1,16,128]{3,2,1,0:T(8,128)S(1)}, f32[19,1,16,128]{3,2,1,0:T(8,128)S(1)}, u32[]{:S(2)}, u32[]{:S(2)}) collective-permute-start(f32[19,1,16,128]{3,2,1,0:T(8,128)S(1)} %get-tuple-element.109), channel_id=1, source_target_pairs={{0,8},{8,16},{16,24},{24,0},{1,9},{9,17},{17,25},{25,1},{2,10},{10... | collective-permute-start | bytes 466952 | tf_op jit(solution)/shard_map/ppermute | solution.py:44
  74.2 4.0 %collective-permute-start.14 = (f32[19,4,1,128]{3,2,1,0:T(1,128)S(1)}, f32[19,4,1,128]{3,2,1,0:T(1,128)S(1)}, u32[]{:S(2)}, u32[]{:S(2)}) collective-permute-start(f32[19,4,1,128]{3,2,1,0:T(1,128)S(1)} %get-tuple-element.102), channel_id=1, source_target_pairs={{4,0},{0,4},{5,1},{1,5},{6,2},{2,6},{7,3},{3,7},{12,8},{8,12},{13,... | collective-permute-start | bytes 116744 | tf_op jit(solution)/shard_map/ppermute | solution.py:47
  75.8 4.0 %collective-permute-start.15 = (f32[19,4,1,128]{3,2,1,0:T(1,128)S(1)}, f32[19,4,1,128]{3,2,1,0:T(1,128)S(1)}, u32[]{:S(2)}, u32[]{:S(2)}) collective-permute-start(f32[19,4,1,128]{3,2,1,0:T(1,128)S(1)} %get-tuple-element.101), channel_id=1, source_target_pairs={{0,4},{4,0},{1,5},{5,1},{2,6},{6,2},{3,7},{7,3},{8,12},{12,8},{9,1... | collective-permute-start | bytes 116744 | tf_op jit(solution)/shard_map/ppermute | solution.py:44
  80.8 1.7 collective-permute-start.16
  81.5 3.6 %collective-permute-start.17 = (f32[19,4,18,1]{0,1,3,2:T(4,128)S(1)}, f32[19,4,18,1]{0,1,3,2:T(4,128)S(1)}, u32[]{:S(2)}, u32[]{:S(2)}) collective-permute-start(f32[19,4,18,1]{0,1,3,2:T(4,128)S(1)} %copy.98), channel_id=1, source_target_pairs={{0,1},{1,2},{2,3},{3,0},{4,5},{5,6},{6,7},{7,4},{8,9},{9,10},{10,1... | collective-permute-start | bytes 16424 | tf_op jit(solution)/shard_map/ppermute | solution.py:44
  87.0 28.7 %collective-permute-start.18 = (f32[19,1,16,128]{3,2,1,0:T(8,128)S(1)}, f32[19,1,16,128]{3,2,1,0:T(8,128)S(1)}, u32[]{:S(2)}, u32[]{:S(2)}) collective-permute-start(f32[19,1,16,128]{3,2,1,0:T(8,128)S(1)} %get-tuple-element.108), channel_id=1, source_target_pairs={{0,8},{8,16},{16,24},{24,0},{1,9},{9,17},{17,25},{25,1},{2,10},{10... | collective-permute-start | bytes 466952 | tf_op jit(solution)/shard_map/ppermute | solution.py:44
  87.5 28.2 %collective-permute-start.19 = (f32[19,1,16,128]{3,2,1,0:T(8,128)S(1)}, f32[19,1,16,128]{3,2,1,0:T(8,128)S(1)}, u32[]{:S(2)}, u32[]{:S(2)}) collective-permute-start(f32[19,1,16,128]{3,2,1,0:T(8,128)S(1)} %get-tuple-element.107), channel_id=1, source_target_pairs={{8,0},{16,8},{24,16},{0,24},{9,1},{17,9},{25,17},{1,25},{10,2},{18... | collective-permute-start | bytes 466952 | tf_op jit(solution)/shard_map/ppermute | solution.py:47
  115.8 4.0 %collective-permute-start.20 = (f32[19,4,1,128]{3,2,1,0:T(1,128)S(1)}, f32[19,4,1,128]{3,2,1,0:T(1,128)S(1)}, u32[]{:S(2)}, u32[]{:S(2)}) collective-permute-start(f32[19,4,1,128]{3,2,1,0:T(1,128)S(1)} %get-tuple-element.100), channel_id=1, source_target_pairs={{0,4},{4,0},{1,5},{5,1},{2,6},{6,2},{3,7},{7,3},{8,12},{12,8},{9,1... | collective-permute-start | bytes 116744 | tf_op jit(solution)/shard_map/ppermute | solution.py:44
  116.4 4.0 %collective-permute-start.21 = (f32[19,4,1,128]{3,2,1,0:T(1,128)S(1)}, f32[19,4,1,128]{3,2,1,0:T(1,128)S(1)}, u32[]{:S(2)}, u32[]{:S(2)}) collective-permute-start(f32[19,4,1,128]{3,2,1,0:T(1,128)S(1)} %get-tuple-element.99), channel_id=1, source_target_pairs={{4,0},{0,4},{5,1},{1,5},{6,2},{2,6},{7,3},{3,7},{12,8},{8,12},{13,... | collective-permute-start | bytes 116744 | tf_op jit(solution)/shard_map/ppermute | solution.py:47
  121.5 3.5 %collective-permute-start.22 = (f32[19,4,18,1]{2,0,3,1:T(8,128)S(1)}, f32[19,4,18,1]{2,0,3,1:T(8,128)S(1)}, u32[]{:S(2)}, u32[]{:S(2)}) collective-permute-start(f32[19,4,18,1]{2,0,3,1:T(8,128)S(1)} %copy.100), channel_id=1, source_target_pairs={{0,1},{1,2},{2,3},{3,0},{4,5},{5,6},{6,7},{7,4},{8,9},{9,10},{10,1... | collective-permute-start | bytes 16424 | tf_op jit(solution)/shard_map/ppermute | solution.py:44
  122.2 3.5 %collective-permute-start.23 = (f32[19,4,18,1]{2,0,3,1:T(8,128)S(1)}, f32[19,4,18,1]{2,0,3,1:T(8,128)S(1)}, u32[]{:S(2)}, u32[]{:S(2)}) collective-permute-start(f32[19,4,18,1]{2,0,3,1:T(8,128)S(1)} %copy.102), channel_id=1, source_target_pairs={{1,0},{2,1},{3,2},{0,3},{5,4},{6,5},{7,6},{4,7},{9,8},{10,9},{11,1... | collective-permute-start | bytes 16424 | tf_op jit(solution)/shard_map/ppermute | solution.py:47
  127.1 81.6 %copy-start.2 = (f32[19,2,16,128]{3,2,1,0:T(8,128)}, f32[19,2,16,128]{3,2,1,0:T(8,128)S(1)}, u32[]{:S(2)}) copy-start(f32[19,2,16,128]{3,2,1,0:T(8,128)S(1)} %constant_dynamic-update-slice_fusion.152) | copy-start | bytes 933892
Sparse Core Ops, SparseCore 0:
  115.8 38.3 reduce-scatter.1
